TPU v7x, 512 devices: a whole 4x8x8 slice. The times are simulated.
512 devices in a mesh: pb: 16 (over y, x_lo), item: 32 (over x_hi, z, core).
Axes of the slice: x: 4 (x_hi: 2, x_lo: 2; x = x_hi * 2 + x_lo), y: 8, z: 8, core: 2. Of those that a mesh axis runs over, the one named last changes fastest.
Arguments:
- queries: bfloat16 [8192, 512], P(('pb', 'item')), may hold values from -2 to 2
- gate_query: bfloat16 [8192, 64], P(('pb', 'item')), may hold values from -6 to 250
- items: bfloat16 [16384, 512], P(('item', 'pb')), may hold values from -2 to 2
- gate_items: bfloat16 [16384, 64], P(('item', 'pb')), may hold values from -6 to 6
- slot_tiles: int32 [16, 192], P('pb', 'item'), may hold values from -1 to 15, as said below
- d_scores: bfloat16 [16, 192, 128, 128], P('pb', 'item'), may hold values from -6 to 6
Outputs:
- grad_queries: bfloat16 [8192, 512], P(('pb', 'item'))
- grad_gate_query: float32 [8192, 64], P(('pb', 'item'))
- grad_items: bfloat16 [16384, 512], P(('item', 'pb'))
- grad_gate_items: float32 [16384, 64], P(('item', 'pb'))
Inputs may be any that keep to these rules, and one draw needn't show every extreme that they name: `slot_tiles`: each device's row of slots names distinct tiles, live ones first and -1 after them. Devices (p, j) and (p, j + 32 / 2) form a pair: either one of them has all 6 slots live and the other exactly one, or both have between 1 and 3 live slots. Device (0, 0) has all 6 live.
All inputs are finite; a program needn't handle non-finite values.
Results may differ from a plain program's by a relative error of at most 0.0049.
Values may be sent and summed in bfloat16 or wider, within the bound.
No kernel may reach another device: no remote copies, remote signals or barrier semaphores. Data moves between devices by JAX's collectives and lax.ppermute only.
A program may use at most 64 MiB of HBM per device.

v0:
```python
import jax
import jax.numpy as jnp
from jax import lax
from jax.sharding import PartitionSpec as P

E = 64
KQ = 8
KI = 8


def tile_grads(query_tile, query_gate, item_tile, item_gate, cotangent):
    extent = query_tile.shape[0]
    query_parts = query_tile.reshape(extent, KQ, E)
    item_parts = item_tile.reshape(extent, KI, E)
    logits = jnp.einsum(
        "qae,ibe->abqi", query_parts, item_parts, preferred_element_type=jnp.float32
    ).reshape(KQ * KI, extent, extent)
    gates = (
        query_gate.astype(jnp.float32).T[:, :, None] + item_gate.astype(jnp.float32).T[:, None, :]
    )
    weights = jax.nn.softmax(gates, axis=0)
    score = jnp.sum(weights * logits, axis=0)
    upstream = cotangent.astype(jnp.float32)[None]
    logit_grad = (upstream * weights).astype(jnp.bfloat16)
    gate_grad = upstream * weights * (logits - score[None])
    logit_parts = logit_grad.reshape(KQ, KI, extent, extent)
    query_grad = jnp.einsum(
        "abqi,ibe->qae", logit_parts, item_parts, preferred_element_type=jnp.float32
    ).reshape(extent, KQ * E)
    item_grad = jnp.einsum(
        "abqi,qae->ibe", logit_parts, query_parts, preferred_element_type=jnp.float32
    ).reshape(extent, KI * E)
    return (query_grad, jnp.sum(gate_grad, axis=2).T, item_grad, jnp.sum(gate_grad, axis=1).T)


def on_device(queries, gate_query, items, gate_items, slot_tiles, d_scores):
    block_queries, block_gates = (
        lax.all_gather(queries, "item", axis=0, tiled=True),
        lax.all_gather(gate_query, "item", axis=0, tiled=True),
    )
    shard_items, shard_gates = (
        lax.all_gather(items, "pb", axis=0, tiled=True),
        lax.all_gather(gate_items, "pb", axis=0, tiled=True),
    )
    extent = d_scores.shape[-1]
    tile_ids = slot_tiles.reshape(-1)
    cotangents = d_scores.reshape(-1, extent, extent)
    slot_count = tile_ids.shape[0]
    item_blocks = shard_items.shape[0] // extent

    def anchors(tile_id):
        safe_id = jnp.maximum(tile_id, 0)
        return (safe_id // item_blocks * extent, safe_id % item_blocks * extent)

    def operands(tile_id):
        query_start, item_start = anchors(tile_id)
        return (
            lax.dynamic_slice_in_dim(block_queries, query_start, extent, 0),
            lax.dynamic_slice_in_dim(block_gates, query_start, extent, 0),
            lax.dynamic_slice_in_dim(shard_items, item_start, extent, 0),
            lax.dynamic_slice_in_dim(shard_gates, item_start, extent, 0),
        )

    def accumulate(current, tile_id, grads):
        query_start, item_start = anchors(tile_id)
        starts = (query_start, query_start, item_start, item_start)
        return tuple(
            (
                lax.dynamic_update_slice_in_dim(
                    total, lax.dynamic_slice_in_dim(total, start, extent, 0) + update, start, 0
                )
                for total, update, start in zip(current, grads, starts)
            )
        )

    totals = (
        jnp.zeros(block_queries.shape, jnp.float32),
        jnp.zeros(block_gates.shape, jnp.float32),
        jnp.zeros(shard_items.shape, jnp.float32),
        jnp.zeros(shard_gates.shape, jnp.float32),
    )

    def home_step(position, current):
        tile_id = tile_ids[position]

        def work(state):
            return accumulate(state, tile_id, tile_grads(*operands(tile_id), cotangents[position]))

        return lax.cond(tile_id >= 0, work, lambda state: state, current)

    totals = lax.fori_loop(0, slot_count, home_step, totals)
    query_sum, query_gate_sum = (
        lax.psum_scatter(totals[0], "item", scatter_dimension=0, tiled=True),
        lax.psum_scatter(totals[1], "item", scatter_dimension=0, tiled=True),
    )
    item_sum, item_gate_sum = (
        lax.psum_scatter(totals[2], "pb", scatter_dimension=0, tiled=True),
        lax.psum_scatter(totals[3], "pb", scatter_dimension=0, tiled=True),
    )
    return (
        query_sum.astype(jnp.bfloat16),
        query_gate_sum,
        item_sum.astype(jnp.bfloat16),
        item_gate_sum,
    )


def solution(mesh):
    return jax.shard_map(
        on_device,
        mesh=mesh,
        in_specs=(
            P(("pb", "item"), None),
            P(("pb", "item"), None),
            P(("item", "pb"), None),
            P(("item", "pb"), None),
            P("pb", "item"),
            P("pb", "item", None, None),
        ),
        out_specs=(
            P(("pb", "item"), None),
            P(("pb", "item"), None),
            P(("item", "pb"), None),
            P(("item", "pb"), None),
        ),
        check_vma=False,
    )
```

profile of v0, /device:TPU:4, one launch (start us, length us, event | category | flops | bytes accessed | tf_op | source)
XLA Modules:
  0.0 665.3 jit_solution(1207350731947987089)
XLA Ops:
  7.2 45.9 %all_gather.13 = bf16[512,64]{1,0:T(8,128)(2,1)S(1)} all-gather(bf16[16,64]{1,0:T(8,128)(2,1)} %param.11), channel_id=1, replica_groups=mesh['pb'=16,'item'=32] {'item'}, dimensions={0}, use_global_device_ids=true | all-gather | bytes 67584 | tf_op jit(solution)/shard_map/all_gather | solution.py:39
  53.3 35.4 %all_gather.14 = bf16[512,64]{1,0:T(8,128)(2,1)S(1)} all-gather(bf16[32,64]{1,0:T(8,128)(2,1)} %param.13), channel_id=1, replica_groups=mesh['pb'=16,'item'=32] {'pb'}, dimensions={0}, use_global_device_ids=true | all-gather | bytes 69632 | tf_op jit(solution)/shard_map/all_gather | solution.py:43
  88.7 0.7 copy.63
  89.4 1.7 copy.60
  91.2 38.1 %all_gather.15 = bf16[512,512]{1,0:T(8,128)(2,1)S(1)} all-gather(bf16[16,512]{1,0:T(8,128)(2,1)} %param.10), channel_id=1, replica_groups=mesh['pb'=16,'item'=32] {'item'}, dimensions={0}, use_global_device_ids=true | all-gather | bytes 540672 | tf_op jit(solution)/shard_map/all_gather | solution.py:38
  129.5 32.8 %all_gather.12 = bf16[512,512]{1,0:T(8,128)(2,1)S(1)} all-gather(bf16[32,512]{1,0:T(8,128)(2,1)} %param.12), channel_id=1, replica_groups=mesh['pb'=16,'item'=32] {'pb'}, dimensions={0}, use_global_device_ids=true | all-gather | bytes 557056 | tf_op jit(solution)/shard_map/all_gather | solution.py:42
  162.5 0.7 broadcast.34.clone
  163.1 0.7 broadcast.34
  164.0 22.5 %while.19 = (s32[]{:T(128)}, f32[512,512]{0,1:T(8,128)S(1)}, f32[512,64]{0,1:T(8,128)}, f32[512,512]{0,1:T(8,128)S(1)}, f32[512,64]{0,1:T(8,128)}, /*index=5*/s3...) while((s32[]{:T(128)}, f32[512,512]{0,1:T(8,128)S(1)}, ...), condition=%wide.region_8.9_spmd, body=%wide.region_0.8_spmd.sunk | while | flops 432128032 | bytes 13894240 | solution.py:91
  165.3 14.8 %conditional.2 = ((f32[512,512]{0,1:T(8,128)S(1)}, f32[512,64]{0,1:T(8,128)}, f32[512,512]{0,1:T(8,128)S(1)}, f32[512,64]{0,1:T(8,128)})) conditional(s32[]{:T(128)} %convert_element_type.27, (f32[512,512]{0,1:T(8,128)S(1)}, f32[512,64]{0,1:T(8,128)}, f32[512,512]{0,1:T(8,128)S(1)}, f32[512,64]{0,1:T(8,128)}) %tuple.50, (s32[]{:T(128)}, ...), branch_computations={%region_1.0_spmd, %region_2.7_spmd} | conditional | flops 432128032 | bytes 13893961 | solution.py:89
  166.0 0.8 bitcast_convert_fusion
  166.8 0.7 convert_bitcast_fusion
  167.5 1.2 add_reduce_fusion
  168.8 1.3 fusion.1
  170.3 1.3 fusion.7
  171.6 1.3 fusion.6
  173.1 1.3 fusion.2
  174.4 2.9 fusion.4
  177.4 1.4 fusion.8
  178.7 1.4 fusion.9
  181.4 0.6 dynamic_slice.46
  182.7 0.6 dynamic_slice.46
  186.5 1.3 copy.65
  187.9 1.4 copy.67
  189.4 1.8 copy.66
  191.2 1.7 copy.68
  193.0 188.1 %reduce-scatter.5.cloned.1.call-done = f32[16,512]{1,0:T(8,128)} async-done(((f32[512,512]{1,0:T(8,128)}), f32[16,512]{1,0:T(8,128)}) %reduce-scatter.5.cloned.1.call-update) | async-done | bytes 32784 | tf_op jit(solution)/shard_map/reduce_scatter | solution.py:93
  381.1 1.4 convert_element_type.21
  382.5 74.6 %reduce-scatter.9.cloned.1.call-done = f32[32,512]{1,0:T(8,128)} async-done(((f32[512,512]{1,0:T(8,128)}), f32[32,512]{1,0:T(8,128)}) %reduce-scatter.9.cloned.1.call-update) | async-done | bytes 65552 | tf_op jit(solution)/shard_map/reduce_scatter | solution.py:97
  457.1 1.5 convert_element_type.22
  458.6 125.6 %reduce-scatter.7.cloned.1.call-done = f32[16,64]{1,0:T(8,128)} async-done(((f32[512,64]{1,0:T(8,128)}), f32[16,64]{1,0:T(8,128)}) %reduce-scatter.7.cloned.1.call-update) | async-done | bytes 4112 | tf_op jit(solution)/shard_map/reduce_scatter | solution.py:94
  584.1 74.6 %reduce-scatter.11.cloned.1.call-done = f32[32,64]{1,0:T(8,128)} async-done(((f32[512,64]{1,0:T(8,128)}), f32[32,64]{1,0:T(8,128)}) %reduce-scatter.11.cloned.1.call-update) | async-done | bytes 8208 | tf_op jit(solution)/shard_map/reduce_scatter | solution.py:98
  (31 shorter events, 3.8 us)
Async XLA Ops:
  7.2 156.9 %copy-start = (s32[1,6]{1,0:T(1,128)S(1)}, s32[1,6]{1,0:T(1,128)}, u32[]{:S(2)}) copy-start(s32[1,6]{1,0:T(1,128)} %param.14) | copy-start | bytes 76
  7.2 373.9 %reduce-scatter.5.cloned.1.call-start = ((), (), s32[]{:S(2)}) async-start(), calls=%async_computation.4 | async-start | bytes 1081344 | tf_op jit(solution)/shard_map/reduce_scatter | solution.py:93
  187.9 269.2 %reduce-scatter.9.cloned.1.call-start = ((), (), s32[]{:S(2)}) async-start(), calls=%async_computation.6 | async-start | bytes 1114112 | tf_op jit(solution)/shard_map/reduce_scatter | solution.py:97
  189.3 394.8 %reduce-scatter.7.cloned.1.call-start = ((), (), s32[]{:S(2)}) async-start(), calls=%async_computation.5 | async-start | bytes 270336 | tf_op jit(solution)/shard_map/reduce_scatter | solution.py:94
  191.1 467.6 %reduce-scatter.11.cloned.1.call-start = ((), (), s32[]{:S(2)}) async-start(), calls=%async_computation.7 | async-start | bytes 278528 | tf_op jit(solution)/shard_map/reduce_scatter | solution.py:98
Sparse Core Ops, SparseCore 0:
  188.0 193.0 reduce-scatter.4
  383.9 73.1 reduce-scatter.8
  462.3 121.8 reduce-scatter.6
  587.4 71.3 reduce-scatter.10
where the time goes:
time: 667 us; the launch traced here: 665 us
  waiting for transfers between devices  463 us (69%)
  blocking collectives  152 us (23%)
  local copies, waits for them, and re-layouts  14.5 us (2%)
  between operations  13.8 us (2%)
  other arithmetic  12.6 us (2%)
    reduce_scatter x1, waiting for transfers between devices, on_device(): lax.psum_scatter(totals[0], 'item', scatter_dimension=0, tiled=True)  188 us
    reduce_scatter x1, waiting for transfers between devices, on_device(): lax.psum_scatter(totals[1], 'item', scatter_dimension=0, tiled=True)  126 us
    reduce_scatter x1, waiting for transfers between devices, on_device(): lax.psum_scatter(totals[2], 'pb', scatter_dimension=0, tiled=True)  74.6 us
    reduce_scatter x1, waiting for transfers between devices, on_device(): lax.psum_scatter(totals[3], 'pb', scatter_dimension=0, tiled=True)  74.6 us
    all_gather x1, blocking collectives, on_device(): lax.all_gather(gate_query, 'item', axis=0, tiled=True)  45.9 us
    all_gather x1, blocking collectives, on_device(): lax.all_gather(queries, 'item', axis=0, tiled=True)  38.1 us
    all_gather x1, blocking collectives, on_device(): lax.all_gather(gate_items, 'pb', axis=0, tiled=True)  35.4 us
    all_gather x1, blocking collectives, on_device(): lax.all_gather(items, 'pb', axis=0, tiled=True)  32.8 us
  transfers between devices with their start and end apart: 4, of which 4 were waited for; matrix products, arithmetic and copies ran while one was open for 1% of the time, Pallas kernels for 0%

commit v1 on v0

--- a/solution.py
+++ b/solution.py
@@ -40,7 +40,15 @@
     )
     shard_items, shard_gates = (
         lax.all_gather(items, "pb", axis=0, tiled=True),
-        lax.all_gather(gate_items, "pb", axis=0, tiled=True),
+        jnp.concatenate(
+            lax.all_to_all(
+                jnp.stack([gate_items for _ in range(lax.axis_size("pb"))]),
+                axis_name="pb",
+                split_axis=0,
+                concat_axis=0,
+            ),
+            axis=0,
+        ),
     )
     extent = d_scores.shape[-1]
     tile_ids = slot_tiles.reshape(-1)

time: 667 us -> 644 us (0.966)
  blocking collectives: 152 us -> 122 us
  starting transfers between devices: 0.16 us -> 8 us
    all_gather x1 -> x0, blocking collectives: 35.4 us -> none  [on_device(): lax.all_gather(gate_items, 'pb', axis=0, tiled=True)]
    all_gather x1, blocking collectives: 38.1 us -> 47.3 us  [on_device(): lax.all_gather(queries, 'item', axis=0, tiled=True)]
    all_gather x1, blocking collectives: 45.9 us -> 37 us  [on_device(): lax.all_gather(gate_query, 'item', axis=0, tiled=True)]
    all_to_all x0 -> x1, starting transfers between devices: none -> 7.84 us  [on_device(): lax.all_to_all(jnp.stack([gate_items for _ in range(lax.axis_size('pb'))]...]
  transfers between devices with their start and end apart: 4 -> 5, of which waited for: 4 -> 4; matrix products, arithmetic and copies ran while one was open for 1% -> 2% of each run, Pallas kernels for 0% -> 0%
where the time goes in v1:
time: 644 us; the launch traced here: 642 us
  waiting for transfers between devices  461 us (72%)
  blocking collectives  122 us (19%)
  local copies, waits for them, and re-layouts  16.1 us (3%)
  between operations  13.8 us (2%)
  other arithmetic  12.6 us (2%)
  starting transfers between devices  8 us (1%)
    reduce_scatter x1, waiting for transfers between devices, on_device(): lax.psum_scatter(totals[0], 'item', scatter_dimension=0, tiled=True)  186 us
    reduce_scatter x1, waiting for transfers between devices, on_device(): lax.psum_scatter(totals[1], 'item', scatter_dimension=0, tiled=True)  125 us
    reduce_scatter x1, waiting for transfers between devices, on_device(): lax.psum_scatter(totals[2], 'pb', scatter_dimension=0, tiled=True)  74.5 us
    reduce_scatter x1, waiting for transfers between devices, on_device(): lax.psum_scatter(totals[3], 'pb', scatter_dimension=0, tiled=True)  74.4 us
    all_gather x1, blocking collectives, on_device(): lax.all_gather(queries, 'item', axis=0, tiled=True)  47.3 us
    all_gather x1, blocking collectives, on_device(): lax.all_gather(items, 'pb', axis=0, tiled=True)  37.7 us
    all_gather x1, blocking collectives, on_device(): lax.all_gather(gate_query, 'item', axis=0, tiled=True)  37 us
  transfers between devices with their start and end apart: 5, of which 4 were waited for; matrix products, arithmetic and copies ran while one was open for 2% of the time, Pallas kernels for 0%

profile of v1, /device:TPU:4, one launch (start us, length us, event | category | flops | bytes accessed | tf_op | source)
XLA Modules:
  0.0 642.3 jit_solution(5147280407762976191)
XLA Ops:
  7.2 0.7 stack.2
  7.9 0.8 reshape.69
  8.7 7.8 %all-to-all-start = ((bf16[16,2,1024]{2,1,0:T(2,128)(2,1)}), bf16[16,2,1024]{2,1,0:T(2,128)(2,1)S(1)}, u32[]{:S(2)}, u32[]{:S(2)}) async-start(bf16[16,2,1024]{2,1,0:T(2,128)(2,1)} %reshape.69), calls=%async_computation | async-start | bytes 131072 | tf_op jit(solution)/shard_map/all_to_all | solution.py:44
  16.5 47.3 %all_gather.11 = bf16[512,512]{1,0:T(8,128)(2,1)S(1)} all-gather(bf16[16,512]{1,0:T(8,128)(2,1)} %param.10), channel_id=1, replica_groups=mesh['pb'=16,'item'=32] {'item'}, dimensions={0}, use_global_device_ids=true | all-gather | bytes 540672 | tf_op jit(solution)/shard_map/all_gather | solution.py:38
  63.9 37.7 %all_gather.9 = bf16[512,512]{1,0:T(8,128)(2,1)S(1)} all-gather(bf16[32,512]{1,0:T(8,128)(2,1)} %param.12), channel_id=1, replica_groups=mesh['pb'=16,'item'=32] {'pb'}, dimensions={0}, use_global_device_ids=true | all-gather | bytes 557056 | tf_op jit(solution)/shard_map/all_gather | solution.py:42
  101.6 37.0 %all_gather.10 = bf16[512,64]{1,0:T(8,128)(2,1)S(1)} all-gather(bf16[16,64]{1,0:T(8,128)(2,1)} %param.11), channel_id=1, replica_groups=mesh['pb'=16,'item'=32] {'item'}, dimensions={0}, use_global_device_ids=true | all-gather | bytes 67584 | tf_op jit(solution)/shard_map/all_gather | solution.py:39
  138.8 1.7 copy.74
  141.1 0.7 copy.77
  141.8 0.6 broadcast.36.clone
  142.5 0.7 broadcast.36
  143.4 22.5 %while.19 = (s32[]{:T(128)}, f32[512,512]{0,1:T(8,128)S(1)}, f32[512,64]{0,1:T(8,128)}, f32[512,512]{0,1:T(8,128)S(1)}, f32[512,64]{0,1:T(8,128)}, /*index=5*/s3...) while((s32[]{:T(128)}, f32[512,512]{0,1:T(8,128)S(1)}, ...), condition=%wide.region_8.9_spmd, body=%wide.region_0.8_spmd.sunk | while | flops 432128032 | bytes 13894240 | solution.py:99
  144.6 14.8 %conditional.2 = ((f32[512,512]{0,1:T(8,128)S(1)}, f32[512,64]{0,1:T(8,128)}, f32[512,512]{0,1:T(8,128)S(1)}, f32[512,64]{0,1:T(8,128)})) conditional(s32[]{:T(128)} %convert_element_type.27, (f32[512,512]{0,1:T(8,128)S(1)}, f32[512,64]{0,1:T(8,128)}, f32[512,512]{0,1:T(8,128)S(1)}, f32[512,64]{0,1:T(8,128)}) %tuple.51, (s32[]{:T(128)}, ...), branch_computations={%region_1.0_spmd, %region_2.7_spmd} | conditional | flops 432128032 | bytes 13893961 | solution.py:97
  145.3 0.8 bitcast_convert_fusion
  146.1 0.7 convert_bitcast_fusion
  146.8 1.2 add_reduce_fusion
  148.1 1.3 fusion.1
  149.6 1.3 fusion.7
  150.9 1.3 fusion.6
  152.5 1.3 fusion.2
  153.8 2.9 fusion.4
  156.7 1.4 fusion.8
  158.1 1.4 fusion.9
  165.8 1.3 copy.79
  167.2 1.4 copy.81
  168.7 1.8 copy.80
  170.5 1.7 copy.82
  172.3 186.4 %reduce-scatter.5.cloned.1.call-done = f32[16,512]{1,0:T(8,128)} async-done(((f32[512,512]{1,0:T(8,128)}), f32[16,512]{1,0:T(8,128)}) %reduce-scatter.5.cloned.1.call-update) | async-done | bytes 32784 | tf_op jit(solution)/shard_map/reduce_scatter | solution.py:101
  358.7 1.4 convert_element_type.21
  360.1 74.5 %reduce-scatter.9.cloned.1.call-done = f32[32,512]{1,0:T(8,128)} async-done(((f32[512,512]{1,0:T(8,128)}), f32[32,512]{1,0:T(8,128)}) %reduce-scatter.9.cloned.1.call-update) | async-done | bytes 65552 | tf_op jit(solution)/shard_map/reduce_scatter | solution.py:105
  434.6 1.5 convert_element_type.22
  436.0 125.3 %reduce-scatter.7.cloned.1.call-done = f32[16,64]{1,0:T(8,128)} async-done(((f32[512,64]{1,0:T(8,128)}), f32[16,64]{1,0:T(8,128)}) %reduce-scatter.7.cloned.1.call-update) | async-done | bytes 4112 | tf_op jit(solution)/shard_map/reduce_scatter | solution.py:102
  561.3 74.4 %reduce-scatter.11.cloned.1.call-done = f32[32,64]{1,0:T(8,128)} async-done(((f32[512,64]{1,0:T(8,128)}), f32[32,64]{1,0:T(8,128)}) %reduce-scatter.11.cloned.1.call-update) | async-done | bytes 8208 | tf_op jit(solution)/shard_map/reduce_scatter | solution.py:106
  (35 shorter events, 5.1 us)
Async XLA Ops:
  7.2 136.2 %copy-start = (s32[1,6]{1,0:T(1,128)S(1)}, s32[1,6]{1,0:T(1,128)}, u32[]{:S(2)}) copy-start(s32[1,6]{1,0:T(1,128)} %param.14) | copy-start | bytes 76
  8.7 132.3 %all-to-all-start = ((bf16[16,2,1024]{2,1,0:T(2,128)(2,1)}), bf16[16,2,1024]{2,1,0:T(2,128)(2,1)S(1)}, u32[]{:S(2)}, u32[]{:S(2)}) async-start(bf16[16,2,1024]{2,1,0:T(2,128)(2,1)} %reshape.69), calls=%async_computation | async-start | bytes 131072 | tf_op jit(solution)/shard_map/all_to_all | solution.py:44
  16.5 342.2 %reduce-scatter.5.cloned.1.call-start = ((), (), s32[]{:S(2)}) async-start(), calls=%async_computation.5 | async-start | bytes 1081344 | tf_op jit(solution)/shard_map/reduce_scatter | solution.py:101
  167.2 267.4 %reduce-scatter.9.cloned.1.call-start = ((), (), s32[]{:S(2)}) async-start(), calls=%async_computation.7 | async-start | bytes 1114112 | tf_op jit(solution)/shard_map/reduce_scatter | solution.py:105
  168.6 392.7 %reduce-scatter.7.cloned.1.call-start = ((), (), s32[]{:S(2)}) async-start(), calls=%async_computation.6 | async-start | bytes 270336 | tf_op jit(solution)/shard_map/reduce_scatter | solution.py:102
  170.5 465.3 %reduce-scatter.11.cloned.1.call-start = ((), (), s32[]{:S(2)}) async-start(), calls=%async_computation.8 | async-start | bytes 278528 | tf_op jit(solution)/shard_map/reduce_scatter | solution.py:106
Sparse Core Ops, SparseCore 0:
  167.3 191.3 reduce-scatter.4
  361.5 73.0 reduce-scatter.8
  439.8 121.5 reduce-scatter.6
  564.6 71.1 reduce-scatter.10
